TPU v7x, 32 devices: a whole 2x2x4 slice. The times are simulated.
32 devices in a mesh: dp: 8 (over z, core), mp: 4 (over y, x).
Axes of the slice: x: 2, y: 2, z: 4, core: 2. Of those that a mesh axis runs over, the one named last changes fastest.
Arguments:
- inputs: bfloat16 [1024, 32768], P('dp', 'mp'), may hold values from -6 to 6
- cotangent: bfloat16 [1024, 32768], P('dp', 'mp'), may hold values from -6 to 6
- first_weight: bfloat16 [128, 2, 256, 256], P('mp', None, 'dp'), may hold values from -0.25 to 0.25
- second_weight: bfloat16 [128, 2, 256, 256], P('mp', None, 'dp'), may hold values from -0.25 to 0.25
- orders: int32 [2, 256], replicated, may hold values from 0 to 255, each once within a row
Outputs:
- input_grad: bfloat16 [1024, 32768], P('dp', 'mp')
- first_grad: float32 [128, 2, 256, 256], P('mp', None, 'dp')
- second_grad: float32 [128, 2, 256, 256], P('mp', None, 'dp')
Inputs may be any that keep to these rules, and one draw needn't show every extreme that they name: Each of the two rows of orders is a permutation of 0 to 255.
All inputs are finite; a program needn't handle non-finite values.
Results may differ from a plain program's by a relative error of at most 0.018.
Values may be sent and summed in bfloat16 or wider, within the bound.
A program may use at most 128 MiB of HBM per device.

v0:
```python
import math

import jax
import jax.numpy as jnp
from jax import lax
from jax.sharding import PartitionSpec as P

B = 256


def partner(value, axis, bit):
    mask = 2**bit
    pairs = [(source, source ^ mask) for source in range(lax.axis_size(axis))]
    return lax.ppermute(value, axis, pairs)


def gelu_tanh(argument):
    return jax.nn.gelu(argument, approximate=True)


def inverse_order(order):
    length = order.shape[0]
    positions = jnp.arange(length, dtype=jnp.int32)
    matches = order[None, :] == positions[:, None]
    return jnp.sum(jnp.where(matches, positions[None, :], 0), axis=1)


def contract(left, right):
    return jnp.einsum("tnk,nkj->tnj", left, right, preferred_element_type=jnp.float32)


def contract_back(left, right):
    return jnp.einsum("tnj,nkj->tnk", left, right, preferred_element_type=jnp.float32)


def outer_sum(left, right):
    return jnp.einsum("tnk,tnj->nkj", left, right, preferred_element_type=jnp.float32)


def shards(inputs, cotangent, first_weight, second_weight, orders):
    tok_rows = inputs.shape[0]
    feature_width = inputs.shape[1]
    local_blocks = feature_width // B
    bit_top = lax.axis_size("mp").bit_length() - 2
    bit_next = bit_top - 1
    grad_scale = 1.0 / math.sqrt(tok_rows * lax.axis_size("dp"))
    order_first = orders[0]
    order_second = orders[1]
    inverse_first = inverse_order(order_first)
    inverse_second = inverse_order(order_second)
    first_full = lax.all_gather(first_weight, "dp", axis=2, tiled=True)
    own_first = first_full[:, 0]
    cross_first = jnp.take(first_full[:, 1], inverse_first, axis=1)
    blocks_in = inputs.reshape(tok_rows, local_blocks, B)
    partner_in = partner(inputs, "mp", bit_top).reshape(tok_rows, local_blocks, B)
    pre_act = contract(blocks_in, own_first) + contract(partner_in, cross_first)
    saved_pre = pre_act.astype(jnp.bfloat16)
    activated = gelu_tanh(pre_act).astype(jnp.bfloat16)
    blocks_cot = cotangent.reshape(tok_rows, local_blocks, B)
    moved_rows = partner(second_weight[:, 1:], "mp", bit_next)
    held_rows = jnp.concatenate([second_weight[:, :1], moved_rows], axis=1)
    second_full = lax.all_gather(held_rows, "dp", axis=2, tiled=True)
    own_second = second_full[:, 0]
    cross_second = jnp.take(second_full[:, 1], inverse_second, axis=1)
    cot_partner = partner(blocks_cot, "mp", bit_next)
    cross_two = contract_back(cot_partner, cross_second).astype(jnp.bfloat16)
    grad_cross = jnp.take(outer_sum(activated, cot_partner), order_second, axis=1)
    act_grad = contract_back(blocks_cot, own_second) + cross_two.astype(jnp.float32)
    pullback = jax.vjp(gelu_tanh, saved_pre.astype(jnp.float32))[1]
    pre_grad = pullback(act_grad)[0].astype(jnp.bfloat16)
    second_term = jnp.stack([outer_sum(activated, blocks_cot), grad_cross], axis=1) * grad_scale
    product_one = contract_back(pre_grad, cross_first).astype(jnp.bfloat16)
    cross_one = partner(product_one, "mp", bit_top)
    input_grad = (contract_back(pre_grad, own_first) + cross_one.astype(jnp.float32)).astype(
        jnp.bfloat16
    )
    input_grad = input_grad.reshape(tok_rows, feature_width)
    first_cross = jnp.take(outer_sum(partner_in, pre_grad), order_first, axis=1)
    first_term = jnp.stack([outer_sum(blocks_in, pre_grad), first_cross], axis=1) * grad_scale
    first_sum, second_sum = (
        lax.psum_scatter(
            first_term.astype(jnp.bfloat16), "dp", scatter_dimension=2, tiled=True
        ).astype(jnp.float32),
        lax.psum_scatter(
            second_term.astype(jnp.bfloat16), "dp", scatter_dimension=2, tiled=True
        ).astype(jnp.float32),
    )
    returned = partner(second_sum[:, 1:].astype(jnp.bfloat16), "mp", bit_next).astype(jnp.float32)
    second_sum = jnp.concatenate([second_sum[:, :1], returned], axis=1)
    return (input_grad, first_sum, second_sum)


def solution(mesh):
    in_specs = (
        P("dp", "mp"),
        P("dp", "mp"),
        P("mp", None, "dp", None),
        P("mp", None, "dp", None),
        P(),
    )
    out_specs = (P("dp", "mp"), P("mp", None, "dp", None), P("mp", None, "dp", None))
    return jax.shard_map(shards, mesh=mesh, in_specs=in_specs, out_specs=out_specs, check_vma=False)
```

profile of v0, /device:TPU:0, one launch (start us, length us, event | category | flops | bytes accessed | tf_op | source)
XLA Modules:
  0.0 375.4 jit_solution(8754357749359150172)
XLA Ops:
  7.2 2.9 copy.92
  11.5 3.0 collective-permute-start
  14.5 11.9 %collective-permute-done = bf16[32,1,32,256]{3,2,0,1:T(8,128)(2,1)S(1)} collective-permute-done((bf16[32,1,32,256]{3,2,0,1:T(8,128)(2,1)S(1)}, bf16[32,1,32,256]{3,2,0,1:T(8,128)(2,1)S(1)}, u32[]{:S(2)}, u32[]{:S(2)}) %collective-permute-start) | collective-permute-done | bytes 524320 | tf_op jit(solution)/shard_map/ppermute | solution.py:14
  27.7 2.4 copy.96
  30.1 1.8 collective-permute-start.2
  31.9 3.3 copy.87
  35.2 2.9 copy.90
  38.1 1.5 collective-permute-start.1
  39.8 55.3 %all-gather.5.cloned.1.call-done = bf16[32,2,256,256]{3,0,1,2:T(8,128)(2,1)} async-done(((bf16[32,2,32,256]{3,0,1,2:T(8,128)(2,1)}), bf16[32,2,256,256]{3,0,1,2:T(8,128)(2,1)}) %all-gather.5.cloned.1.call-update) | async-done | bytes 8388624 | tf_op jit(solution)/shard_map/all_gather | solution.py:51
  95.1 6.0 %slice_bitcast_fusion = (bf16[32,256,256]{2,0,1:T(8,128)(2,1)}, bf16[32,1,256,256]{3,0,1,2:T(8,128)(2,1)}) fusion(bf16[32,2,256,256]{3,0,1,2:T(8,128)(2,1)} %all-gather.5.cloned.1.call-done), kind=kLoop, calls=%fused_computation.32 | loop fusion | bytes 16777216 | tf_op jit(solution)/shard_map/squeeze | solution.py:53
  101.0 7.8 %copy.130 = bf16[32,1,256,256]{2,3,0,1:T(8,128)(2,1)} copy(bf16[32,1,256,256]{3,0,1,2:T(8,128)(2,1)} %get-tuple-element.18) | data formatting | bytes 8388608
  108.8 5.0 %gather_fusion.1 = bf16[256,32,256]{2,1,0:T(8,128)(2,1)} fusion(bf16[32,256,256]{2,0,1:T(8,128)(2,1)} %get-tuple-element.17, s32[1024]{0:T(1024)S(1)} %pad_clamp_fusion.2), kind=kCustom, calls=%fused_computation.2.clone | custom fusion | bytes 8389632 | tf_op jit(solution)/shard_map/jit(_take)/gather | solution.py:53
  113.8 3.4 select_bitcast_fusion.2
  119.4 6.9 %fusion.32 = f32[32,256,128]{2,1,0:T(8,128)S(1)} fusion(f32[32,256,128]{2,1,0:T(8,128)S(1)} %fusion.23, bf16[128,32,256]{0,2,1:T(8,128)(2,1)} %bitcast.10, bf16[32,256,256]{2,0,1:T(8,128)(2,1)S(1)} %select_bitcast_fusion.2), kind=kOutput, calls=%fused_computation.56 | convolution fusion | flops 537919488 | bytes 14680064 | tf_op jit(solution)/shard_map/tnk,nkj->tnj/dot_general | solution.py:29
  126.3 2.1 copy-done
  128.4 3.1 fusion.41
  131.4 8.3 %copy.112 = f32[32,256,256]{2,0,1:T(8,128)} copy(f32[32,256,256]{2,1,0:T(8,128)S(1)} %fusion.41) | data formatting | bytes 16777216 | tf_op jit(solution)/shard_map/tnk,tnj->nkj/dot_general | solution.py:37
  139.7 7.7 %gather_fusion.3 = f32[256,32,256]{2,1,0:T(8,128)} fusion(f32[32,256,256]{2,0,1:T(8,128)} %copy.112, s32[1024]{0:T(1024)S(1)} %pad_clamp_fusion), kind=kCustom, calls=%fused_computation.3.clone | custom fusion | bytes 16778240 | tf_op jit(solution)/shard_map/jit(_take)/gather | solution.py:67
  147.4 10.0 %copy.113 = f32[256,32,256]{0,2,1:T(8,128)} copy(f32[256,32,256]{2,1,0:T(8,128)} %gather_fusion.3) | data formatting | bytes 16777216 | tf_op jit(solution)/shard_map/jit(_take)/gather | solution.py:67
  157.4 4.0 %convolution_bitcast_fusion = f32[32,1,256,256]{2,3,0,1:T(8,128)S(1)} fusion(bf16[128,32,256]{0,2,1:T(8,128)(2,1)S(1)} %bitcast.86, f32[32,256,128]{2,1,0:T(8,128)} %copy-done), kind=kOutput, calls=%fused_computation.53 | convolution fusion | flops 546308096 | bytes 14680064 | tf_op jit(solution)/shard_map/tnk,tnj->nkj/dot_general | solution.py:37
  161.4 4.0 %select_bitcast_fusion = f32[32,1,256,256]{2,3,0,1:T(8,128)S(1)} fusion(f32[256,32,256]{0,2,1:T(8,128)} %copy.113, pred[256]{0:T(512)(128)(4,1)S(1)} %compare_and_fusion), kind=kLoop, calls=%fused_computation.8 | loop fusion | flops 2097152 | bytes 16777472 | tf_op jit(solution)/shard_map/stack | solution.py:71
  165.4 4.4 %fusion.1 = bf16[32,2,256,256]{2,3,0,1:T(8,128)(2,1)} fusion(f32[32,1,256,256]{2,3,0,1:T(8,128)S(1)} %select_bitcast_fusion, f32[32,1,256,256]{2,3,0,1:T(8,128)S(1)} %convolution_bitcast_fusion), kind=kLoop, calls=%fused_computation.7 | loop fusion | flops 12582912 | bytes 25165824 | tf_op jit(solution)/shard_map/convert_element_type | solution.py:85
  169.9 14.6 %copy.114 = bf16[32,2,256,256]{3,0,1,2:T(8,128)(2,1)} copy(bf16[32,2,256,256]{2,3,0,1:T(8,128)(2,1)} %fusion.1) | data formatting | bytes 16777216 | tf_op jit(solution)/shard_map/convert_element_type | solution.py:85
  184.8 2.5 slice_bitcast_fusion.1
  187.3 4.4 %copy.89 = bf16[32,256,256]{2,0,1:T(8,128)(2,1)} copy(bf16[32,256,256]{2,1,0:T(8,128)(2,1)S(1)} %slice_bitcast_fusion.1) | data formatting | bytes 8388608 | tf_op jit(solution)/shard_map/squeeze | solution.py:64
  191.6 5.0 %gather_fusion = bf16[256,32,256]{2,1,0:T(8,128)(2,1)} fusion(bf16[32,256,256]{2,0,1:T(8,128)(2,1)} %copy.89, s32[1024]{0:T(1024)S(1)} %pad_clamp_fusion.3), kind=kCustom, calls=%fused_computation.clone | custom fusion | bytes 8389632 | tf_op jit(solution)/shard_map/jit(_take)/gather | solution.py:64
  196.6 2.9 select_bitcast_fusion.3
  199.6 4.4 %fusion.26 = bf16[32,256,128]{2,1,0:T(8,128)(2,1)S(1)} fusion(bf16[128,32,256]{2,0,1:T(8,128)(2,1)} %collective-permute-done.1, bf16[32,256,256]{2,0,1:T(8,128)(2,1)S(1)} %select_bitcast_fusion.3), kind=kOutput, calls=%fused_computation.45 | convolution fusion | flops 536870912 | bytes 8388608 | tf_op jit(solution)/shard_map/tnj,nkj->tnk/dot_general | solution.py:33
  203.9 5.8 %fusion.5 = bf16[128,32,256]{0,2,1:T(8,128)(2,1)S(1)} fusion(f32[32,256,128]{2,1,0:T(8,128)S(1)} %copy-done.1, bf16[32,256,128]{2,1,0:T(8,128)(2,1)S(1)} %fusion.26, bf16[128,32,256]{0,2,1:T(8,128)(2,1)S(1)} %bitcast.87, bf16[32,2,256,256]{3,2,0,1:T(8,128)(2,1)} %all-gather.3.cloned.1.call-done), kind=kOutput, calls=%fused_computation.18 | convolution fusion | flops 562036736 | bytes 14680064 | tf_op jit(solution)/shard_map/tnj,nkj->tnk/dot_general | solution.py:33
  209.7 6.1 %convolution_bitcast_fusion.1 = f32[32,256,256]{1,2,0:T(8,128)} fusion(bf16[128,32,256]{0,2,1:T(8,128)(2,1)S(1)} %fusion.5, bf16[128,32,256]{0,2,1:T(8,128)(2,1)} %bitcast.10), kind=kOutput, calls=%fused_computation.54 | convolution fusion | flops 536870912 | bytes 12582912 | tf_op jit(solution)/shard_map/tnk,tnj->nkj/dot_general | solution.py:37
  215.8 10.3 %copy.107 = f32[32,256,256]{2,0,1:T(8,128)} copy(f32[32,256,256]{1,2,0:T(8,128)} %convolution_bitcast_fusion.1) | data formatting | bytes 16777216 | tf_op jit(solution)/shard_map/tnk,tnj->nkj/dot_general | solution.py:37
  226.2 7.8 %gather_fusion.2 = f32[256,32,256]{2,1,0:T(8,128)} fusion(f32[32,256,256]{2,0,1:T(8,128)} %copy.107, s32[1024]{0:T(1024)S(1)} %pad_clamp_fusion.1), kind=kCustom, calls=%fused_computation.1.clone | custom fusion | bytes 16778240 | tf_op jit(solution)/shard_map/jit(_take)/gather | solution.py:78
  234.0 10.0 %copy.108 = f32[256,32,256]{0,2,1:T(8,128)} copy(f32[256,32,256]{2,1,0:T(8,128)} %gather_fusion.2) | data formatting | bytes 16777216 | tf_op jit(solution)/shard_map/jit(_take)/gather | solution.py:78
  244.0 2.9 convolution_bitcast_fusion.2
  246.9 4.0 %select_bitcast_fusion.1 = f32[32,1,256,256]{2,3,0,1:T(8,128)S(1)} fusion(f32[256,32,256]{0,2,1:T(8,128)} %copy.108, pred[256]{0:T(512)(128)(4,1)S(1)} %compare_and_fusion.1), kind=kLoop, calls=%fused_computation.9 | loop fusion | flops 2097152 | bytes 16777472 | tf_op jit(solution)/shard_map/stack | solution.py:79
  250.9 4.5 %fusion = bf16[32,2,256,256]{2,3,0,1:T(8,128)(2,1)} fusion(f32[32,1,256,256]{2,3,0,1:T(8,128)S(1)} %select_bitcast_fusion.1, f32[32,1,256,256]{2,3,0,1:T(8,128)S(1)} %convolution_bitcast_fusion.2), kind=kLoop, calls=%fused_computation.5 | loop fusion | flops 12582912 | bytes 25165824 | tf_op jit(solution)/shard_map/convert_element_type | solution.py:82
  255.5 14.9 %copy.109 = bf16[32,2,256,256]{3,0,1,2:T(8,128)(2,1)} copy(bf16[32,2,256,256]{2,3,0,1:T(8,128)(2,1)} %fusion) | data formatting | bytes 16777216 | tf_op jit(solution)/shard_map/convert_element_type | solution.py:82
  270.3 6.2 %convert_bitcast_fusion = bf16[128,32,256]{2,0,1:T(8,128)(2,1)} fusion(bf16[128,32,256]{0,2,1:T(8,128)(2,1)S(1)} %fusion.5, bf16[32,256,256]{2,0,1:T(8,128)(2,1)} %copy-done.2), kind=kOutput, calls=%fused_computation.59 | convolution fusion | flops 537919488 | bytes 8388608 | tf_op jit(solution)/shard_map/tnj,nkj->tnk/dot_general | solution.py:33
  276.5 1.6 collective-permute-start.3
  278.1 1.4 fusion.44
  279.8 1.4 collective-permute-start.4
  281.3 43.4 %collective-permute-done.3 = bf16[128,32,256]{2,0,1:T(8,128)(2,1)} collective-permute-done((bf16[128,32,256]{2,0,1:T(8,128)(2,1)}, bf16[128,32,256]{2,0,1:T(8,128)(2,1)}, u32[]{:S(2)}, u32[]{:S(2)}) %collective-permute-start.3) | collective-permute-done | bytes 2097184 | tf_op jit(solution)/shard_map/ppermute | solution.py:14
  324.6 5.2 %fusion.20 = bf16[128,32,256]{2,0,1:T(8,128)(2,1)} fusion(bf16[128,32,256]{2,0,1:T(8,128)(2,1)} %collective-permute-done.3, bf16[128,32,256]{0,2,1:T(8,128)(2,1)S(1)} %fusion.5, bf16[32,1,256,256]{2,3,0,1:T(8,128)(2,1)} %copy.130), kind=kOutput, calls=%fused_computation.37 | convolution fusion | flops 540016640 | bytes 10485760 | tf_op jit(solution)/shard_map/tnj,nkj->tnk/dot_general | solution.py:33
  329.8 3.2 copy.104
  333.1 2.9 copy.117
  336.3 26.7 %reduce-scatter.3.cloned.1.call-done = bf16[32,2,32,256]{3,0,1,2:T(8,128)(2,1)} async-done(((bf16[32,2,256,256]{3,0,1,2:T(8,128)(2,1)}), bf16[32,2,32,256]{3,0,1,2:T(8,128)(2,1)}) %reduce-scatter.3.cloned.1.call-update) | async-done | bytes 1048592 | tf_op jit(solution)/shard_map/reduce_scatter | solution.py:81
  362.9 3.2 copy.118
  366.1 2.5 maximum_convert_fusion
  (50 shorter events, 5.7 us)
Async XLA Ops:
  7.2 20.5 %copy-start.6 = (bf16[128,8192]{1,0:T(8,128)(2,1)S(1)}, bf16[128,8192]{1,0:T(8,128)(2,1)}, u32[]{:S(2)}) copy-start(bf16[128,8192]{1,0:T(8,128)(2,1)} %param.9) | copy-start | bytes 6291460
  7.2 87.9 %all-gather.5.cloned.1.call-start = ((), (), s32[]{:S(2)}) async-start(), calls=%async_computation.3 | async-start | bytes 9437184 | tf_op jit(solution)/shard_map/all_gather | solution.py:51
  10.2 174.6 %all-gather.3.cloned.1.call-start = ((), (), s32[]{:S(2)}) async-start(), calls=%async_computation.2 | async-start | bytes 9437184 | tf_op jit(solution)/shard_map/all_gather | solution.py:62
  11.5 15.0 %collective-permute-start = (bf16[32,1,32,256]{3,2,0,1:T(8,128)(2,1)S(1)}, bf16[32,1,32,256]{3,2,0,1:T(8,128)(2,1)S(1)}, u32[]{:S(2)}, u32[]{:S(2)}) collective-permute-start(bf16[32,1,32,256]{3,2,0,1:T(8,128)(2,1)S(1)} %get-tuple-element.22), channel_id=1, source_target_pairs={{0,1},{1,0},{2,3},{3,2},{4,5},{5,4},{6,7},{7,6},{8,9},{9,8},{10,11... | collective-permute-start | bytes 1572872 | tf_op jit(solution)/shard_map/ppermute | solution.py:14
  27.6 250.5 %reduce-scatter.5.cloned.1.call-start = ((), (), s32[]{:S(2)}) async-start(), calls=%async_computation.5 | async-start | bytes 9437184 | tf_op jit(solution)/shard_map/reduce_scatter | solution.py:84
  30.1 9.4 %copy-start.8 = (s32[2,256]{1,0:T(2,128)S(1)}, s32[2,256]{1,0:T(2,128)}, u32[]{:S(2)}) copy-start(s32[2,256]{1,0:T(2,128)} %param.13) | copy-start | bytes 6148
  30.1 89.3 %collective-permute-start.2 = (bf16[128,8192]{0,1:T(8,128)(2,1)}, bf16[128,8192]{0,1:T(8,128)(2,1)}, u32[]{:S(2)}, u32[]{:S(2)}) collective-permute-start(bf16[128,8192]{0,1:T(8,128)(2,1)} %copy.96), channel_id=1, source_target_pairs={{0,2},{1,3},{2,0},{3,1},{4,6},{5,7},{6,4},{7,5},{8,10},{9,11},{10,... | collective-permute-start | bytes 6291464 | tf_op jit(solution)/shard_map/ppermute | solution.py:14
  35.2 122.3 %copy-start.4 = (bf16[128,8192]{0,1:T(8,128)(2,1)}, bf16[128,8192]{0,1:T(8,128)(2,1)S(1)}, u32[]{:S(2)}) copy-start(bf16[128,8192]{0,1:T(8,128)(2,1)S(1)} %copy.87) | copy-start | bytes 6291460
  38.1 88.2 %collective-permute-start.1 = (bf16[128,32,256]{2,0,1:T(8,128)(2,1)}, bf16[128,32,256]{2,0,1:T(8,128)(2,1)}, u32[]{:S(2)}, u32[]{:S(2)}) collective-permute-start(bf16[128,32,256]{2,0,1:T(8,128)(2,1)} %copy.90), channel_id=1, source_target_pairs={{0,1},{1,0},{2,3},{3,2},{4,5},{5,4},{6,7},{7,6},{8,9},{9,8},{10,11... | collective-permute-start | bytes 6291464 | tf_op jit(solution)/shard_map/ppermute | solution.py:14
  113.8 3.6 copy-start.3
  113.8 4.3 %copy-start.7 = (bf16[128,8192]{1,0:T(8,128)(2,1)S(1)}, bf16[128,8192]{1,0:T(8,128)(2,1)}, u32[]{:S(2)}) copy-start(bf16[128,8192]{1,0:T(8,128)(2,1)} %param.9) | copy-start | bytes 6291460
  117.3 2.1 copy-start.2
  126.3 2.1 copy-start
  184.5 178.4 %reduce-scatter.3.cloned.1.call-start = ((), (), s32[]{:S(2)}) async-start(), calls=%async_computation.4 | async-start | bytes 9437184 | tf_op jit(solution)/shard_map/reduce_scatter | solution.py:81
  199.5 4.4 %copy-start.1 = (f32[32,256,128]{2,1,0:T(8,128)S(1)}, f32[32,256,128]{2,1,0:T(8,128)}, u32[]{:S(2)}) copy-start(f32[32,256,128]{2,1,0:T(8,128)} %copy-done) | copy-start | bytes 12582916
  199.6 4.4 %copy-start.5 = (bf16[128,8192]{0,1:T(8,128)(2,1)S(1)}, bf16[128,8192]{0,1:T(8,128)(2,1)}, u32[]{:S(2)}) copy-start(bf16[128,8192]{0,1:T(8,128)(2,1)} %copy-done.4) | copy-start | bytes 6291460
  276.5 48.1 %collective-permute-start.3 = (bf16[128,32,256]{2,0,1:T(8,128)(2,1)}, bf16[128,32,256]{2,0,1:T(8,128)(2,1)}, u32[]{:S(2)}, u32[]{:S(2)}) collective-permute-start(bf16[128,32,256]{2,0,1:T(8,128)(2,1)} %convert_bitcast_fusion), channel_id=1, source_target_pairs={{0,2},{1,3},{2,0},{3,1},{4,6},{5,7},{6,4},{7,5},{8,10},{9,11},{10,... | collective-permute-start | bytes 6291464 | tf_op jit(solution)/shard_map/ppermute | solution.py:14
  279.8 86.3 %collective-permute-start.4 = (bf16[32,1,32,256]{3,2,1,0:T(8,128)(2,1)S(1)}, bf16[32,1,32,256]{3,2,1,0:T(8,128)(2,1)}, u32[]{:S(2)}, u32[]{:S(2)}) collective-permute-start(bf16[32,1,32,256]{3,2,1,0:T(8,128)(2,1)S(1)} %copy.115), channel_id=1, source_target_pairs={{0,1},{1,0},{2,3},{3,2},{4,5},{5,4},{6,7},{7,6},{8,9},{9,8},{10,11... | collective-permute-start | bytes 1572872 | tf_op jit(solution)/shard_map/ppermute | solution.py:14
Sparse Core Ops, SparseCore 0:
  10.3 84.7 all-gather.4
  96.7 80.5 all-gather.2
  184.6 88.0 reduce-scatter.4
  274.9 87.9 reduce-scatter.2
where the time goes:
time: 381 us; the launch traced here: 375 us
  local copies, waits for them, and re-layouts  141 us (37%)
  waiting for transfers between devices  137 us (36%)
  matrix products  45.7 us (12%)
  other arithmetic  27.3 us (7%)
  between operations  14.4 us (4%)
  starting transfers between devices  9.5 us (2%)
    all_gather x1, waiting for transfers between devices, shards(): first_full = lax.all_gather(first_weight, 'dp', axis=2, tiled=True)  55.3 us
    ppermute x5, waiting for transfers between devices, partner(): return lax.ppermute(value, axis, pairs)  55.3 us
    unnamed x25, local copies, waits for them, and re-layouts  26.7 us
    reduce_scatter x1, waiting for transfers between devices, shards(): lax.psum_scatter(first_term.astype(jnp.bfloat16), 'dp', scatter_dimension...  26.7 us
    dot_general x4, matrix products, contract_back(): jnp.einsum('tnj,nkj->tnk', left, right, preferred_element_type=jnp.float32)  21.5 us
    dot_general x2, local copies, waits for them, and re-layouts, outer_sum(): jnp.einsum('tnk,tnj->nkj', left, right, preferred_element_type=jnp.float32)  18.6 us
    gather x2, local copies, waits for them, and re-layouts, shards(): first_cross = jnp.take(outer_sum(partner_in, pre_grad), order_first, axis=1)  17.8 us
    gather x2, local copies, waits for them, and re-layouts, shards(): jnp.take(outer_sum(activated, cot_partner), order_second, axis=1)  17.7 us
  transfers between devices with their start and end apart: 9, of which 4 were waited for; matrix products, arithmetic and copies ran while one was open for 55% of the time, Pallas kernels for 0%

commit v1 on v0

v1 whole, which is shorter than its diff:
```python
import functools
import math

import jax
import jax.numpy as jnp
from jax import lax
from jax.experimental import pallas as pl
from jax.experimental.pallas import tpu as pltpu
from jax.sharding import PartitionSpec as P

B = 256
MESH = pl.DeviceIdType.MESH
ANY = pl.BlockSpec(memory_space=pl.ANY)
NT = (((1,), (1,)), ((), ()))
TN = (((0,), (0,)), ((), ()))


class Plan:
    def __init__(self, dp, mp, local_blocks):
        self.dp, self.mp, self.nb = dp, mp, local_blocks
        self.low = mp // 4
        g = max(1, dp // 2)
        while local_blocks % (4 * g):
            g //= 2
        self.g, self.groups = g, dp // g
        self.nq = local_blocks // (4 * g)

    def here(self):
        d, m = lax.axis_index("dp"), lax.axis_index("mp")
        return d, d // self.g, d % self.g, m // self.low, m % self.low


def greet(plan, d, h, lo):
    barrier = pltpu.get_barrier_semaphore()
    others = 4 * plan.dp
    me = d * 4 + h
    for k in range(1, others):
        t = (me + k) % others
        pl.semaphore_signal(
            barrier, inc=1, device_id=(t // 4, (t % 4) * plan.low + lo), device_id_type=MESH
        )
    pl.semaphore_wait(barrier, others - 1)


def run(remote, local):
    for c in remote:
        c.start()
    for c in local:
        c.start()
    for c in local:
        c.wait()
    for c in remote:
        c.wait()


def bring(plan, x, c, w1, w2, xo, co, w1o, w2o, ts, tr, ws, wr, ls):
    d, gi, r, h, lo = plan.here()
    tok = x.shape[0]
    rows = w1.shape[2]
    wide = plan.nq * B
    greet(plan, d, h, lo)

    def tokens(a, src, dst, k):
        n = 4 * plan.g
        me = r * 4 + h
        t = (me + k) % n
        s = src.at[:, pl.ds(pl.multiple_of(t * wide, wide), wide)]
        e = dst.at[h, pl.ds(pl.multiple_of(r * tok, tok), tok)]
        if k == 0:
            return pltpu.make_async_copy(s, e, ls.at[a])
        return pltpu.make_async_remote_copy(
            s, e, ts.at[a, k], tr.at[a, k],
            device_id=(gi * plan.g + t // 4, (t % 4) * plan.low + lo), device_id_type=MESH,
        )

    def weights(a, src, dst, k):
        n = 4 * plan.dp
        me = d * 4 + h
        t = (me + k) % n
        td, th = t // 4, t % 4
        o = (td % plan.g) * 4 + th
        s = src.at[pl.ds(o * plan.nq, plan.nq)]
        e = dst.at[h, :, :, pl.ds(pl.multiple_of(d * rows, rows), rows)]
        if k == 0:
            return pltpu.make_async_copy(s, e, ls.at[2 + a])
        return pltpu.make_async_remote_copy(
            s, e, ws.at[a, k], wr.at[a, k],
            device_id=(td, th * plan.low + lo), device_id_type=MESH,
        )

    remote = []
    for k in range(1, 4 * plan.dp):
        remote += [weights(0, w1, w1o, k), weights(1, w2, w2o, k)]
        if k < 4 * plan.g:
            remote += [tokens(0, x, xo, k), tokens(1, c, co, k)]
    local = [tokens(0, x, xo, 0), tokens(1, c, co, 0), weights(0, w1, w1o, 0), weights(1, w2, w2o, 0)]
    run(remote, local)


def send_back(plan, ig, gf, gs, igo, gfo, gso, ts, tr, ws, wr, ls):
    d, gi, r, h, lo = plan.here()
    tok = igo.shape[0]
    rows = gfo.shape[3]
    wide = plan.nq * B
    greet(plan, d, h, lo)
    me_o = r * 4 + h

    def tokens(k):
        n = 4 * plan.g
        t = (me_o + k) % n
        s = ig.at[t % 4, pl.ds(pl.multiple_of((t // 4) * tok, tok), tok)]
        e = igo.at[:, pl.ds(pl.multiple_of(me_o * wide, wide), wide)]
        if k == 0:
            return pltpu.make_async_copy(s, e, ls.at[0])
        return pltpu.make_async_remote_copy(
            s, e, ts.at[k], tr.at[k],
            device_id=(gi * plan.g + t // 4, (t % 4) * plan.low + lo), device_id_type=MESH,
        )

    def grads(a, src, dst, k):
        n = 4 * plan.dp
        t = (d * 4 + h + k) % n
        td, th = t // 4, t % 4
        s = src.at[th, :, :, pl.ds(pl.multiple_of(td * rows, rows), rows)]
        e = dst.at[gi, pl.ds(me_o * plan.nq, plan.nq)]
        if k == 0:
            return pltpu.make_async_copy(s, e, ls.at[1 + a])
        return pltpu.make_async_remote_copy(
            s, e, ws.at[a, k], wr.at[a, k],
            device_id=(td, th * plan.low + lo), device_id_type=MESH,
        )

    remote = []
    for k in range(1, 4 * plan.dp):
        remote += [grads(0, gf, gfo, k), grads(1, gs, gso, k)]
        if k < 4 * plan.g:
            remote += [tokens(k)]
    local = [tokens(0), grads(0, gf, gfo, 0), grads(1, gs, gso, 0)]
    run(remote, local)


def dot(left, right, dims=(((1,), (0,)), ((), ()))):
    return lax.dot_general(left, right, dims, preferred_element_type=jnp.float32)


def factors(scale, order, x, c, w1, w2, ig, gf, gs, w1p, w2p, act, pre):
    bf = jnp.bfloat16
    place = lax.broadcasted_iota(jnp.int32, (B, B), 0)
    spread_one = (place == order[0:1, :]).astype(jnp.float32).astype(bf)
    spread_two = (place == order[1:2, :]).astype(jnp.float32).astype(bf)
    root = math.sqrt(2.0 / math.pi)
    for h in range(4):
        w1p[h] = dot(spread_one, w1[h, 0, 1]).astype(bf)
        w2p[h] = dot(spread_two, w2[h, 0, 1]).astype(bf)
    for h in range(4):
        p, q = h ^ 2, h ^ 1
        v = dot(x[h], w1[h, 0, 0]) + dot(x[p], w1p[h])
        up = dot(c[h], w2[h, 0, 0], NT) + dot(c[q], w2p[q], NT)
        v2 = v * v
        t = jnp.tanh(root * v * (1.0 + 0.044715 * v2))
        half = 0.5 + 0.5 * t
        act[h] = (v * half).astype(bf)
        slope = half + (0.5 * root) * v * (1.0 - t * t) * (1.0 + (3 * 0.044715) * v2)
        pre[h] = (up * slope).astype(bf)
    for h in range(4):
        p, q = h ^ 2, h ^ 1
        ig[h] = (dot(pre[h], w1[h, 0, 0], NT) + dot(pre[p], w1p[p], NT)).astype(bf)
        gf[h, 0, 0] = (dot(x[h], pre[h], TN) * scale).astype(bf)
        cross = (dot(x[p], pre[h], TN) * scale).astype(bf)
        gf[h, 0, 1] = dot(spread_one, cross, TN).astype(bf)
        gs[h, 0, 0] = (dot(act[h], c[h], TN) * scale).astype(bf)
        cross = (dot(act[q], c[h], TN) * scale).astype(bf)
        gs[h, 0, 1] = dot(spread_two, cross, TN).astype(bf)


def shards(plan, inputs, cotangent, first_weight, second_weight, orders):
    tok, width = inputs.shape
    rows = first_weight.shape[2]
    bf = jnp.bfloat16
    all_tok = plan.g * tok
    nq = plan.nq
    scale = 1.0 / math.sqrt(tok * plan.dp)
    toks = jax.ShapeDtypeStruct((4, all_tok, nq * B), bf)
    mats = jax.ShapeDtypeStruct((4, nq, 2, B, B), bf)
    dma = pltpu.SemaphoreType.DMA
    n_t, n_w = 4 * plan.g, 4 * plan.dp
    x, c, w1, w2 = pl.pallas_call(
        functools.partial(bring, plan),
        out_shape=(toks, toks, mats, mats),
        in_specs=[ANY] * 4,
        out_specs=(ANY,) * 4,
        scratch_shapes=[dma((2, n_t)), dma((2, n_t)), dma((2, n_w)), dma((2, n_w)), dma((4,))],
        compiler_params=pltpu.CompilerParams(collective_id=0, has_side_effects=True),
        name="bring",
    )(inputs, cotangent, first_weight, second_weight)
    tok_spec = pl.BlockSpec((4, all_tok, B), lambda i: (0, 0, i))
    mat_spec = pl.BlockSpec((4, 1, 2, B, B), lambda i: (0, i, 0, 0, 0))
    ig, gf, gs = pl.pallas_call(
        functools.partial(factors, scale),
        out_shape=(toks, mats, mats),
        grid=(nq,),
        in_specs=[pl.BlockSpec((2, B), lambda i: (0, 0)), tok_spec, tok_spec, mat_spec, mat_spec],
        out_specs=(tok_spec, mat_spec, mat_spec),
        scratch_shapes=[
            pltpu.VMEM((4, B, B), bf),
            pltpu.VMEM((4, B, B), bf),
            pltpu.VMEM((4, all_tok, B), bf),
            pltpu.VMEM((4, all_tok, B), bf),
        ],
        compiler_params=pltpu.CompilerParams(vmem_limit_bytes=56 * 2**20),
        name="factors",
    )(orders, x, c, w1, w2)
    part = jax.ShapeDtypeStruct((plan.groups, plan.nb, 2, rows, B), bf)
    input_grad, first, second = pl.pallas_call(
        functools.partial(send_back, plan),
        out_shape=(jax.ShapeDtypeStruct((tok, width), bf), part, part),
        in_specs=[ANY] * 3,
        out_specs=(ANY,) * 3,
        scratch_shapes=[dma((n_t,)), dma((n_t,)), dma((2, n_w)), dma((2, n_w)), dma((3,))],
        compiler_params=pltpu.CompilerParams(collective_id=1, has_side_effects=True),
        name="send_back",
    )(ig, gf, gs)
    total = lambda parts: jnp.sum(parts.astype(jnp.float32), axis=0)
    return input_grad, total(first), total(second)


def solution(mesh):
    in_specs = (
        P("dp", "mp"),
        P("dp", "mp"),
        P("mp", None, "dp", None),
        P("mp", None, "dp", None),
        P(),
    )
    out_specs = (P("dp", "mp"), P("mp", None, "dp", None), P("mp", None, "dp", None))

    def body(inputs, *rest):
        plan = Plan(mesh.shape["dp"], mesh.shape["mp"], inputs.shape[1] // B)
        return shards(plan, inputs, *rest)

    return jax.shard_map(body, mesh=mesh, in_specs=in_specs, out_specs=out_specs, check_vma=False)
```

time: 381 us -> 298 us (0.78)
  the two profiles are of different devices: /device:TPU:0 before, /device:TPU:31 now
where the time goes in v1:
time: 298 us
  Pallas kernels  290 us (97%)
  other arithmetic  5.88 us (2%)
    pallas_call x1, Pallas kernels, shards(): pl.pallas_call(functools.partial(bring, plan), out_shape=(toks, toks, mat...  161 us
    pallas_call x1, Pallas kernels, shards(): pl.pallas_call(functools.partial(send_back, plan), out_shape=(jax.ShapeDt...  115 us
    pallas_call x1, Pallas kernels, shards(): pl.pallas_call(functools.partial(factors, scale), out_shape=(toks, mats,...  14.1 us

profile of v1, /device:TPU:31, one launch (start us, length us, event | category | flops | bytes accessed | tf_op | source)
XLA Modules:
  0.0 298.2 jit_solution(3001033117425851953)
XLA Ops:
  0.6 161.0 %bring.1 = (bf16[4,512,512]{2,1,0:T(8,128)(2,1)}, bf16[4,512,512]{2,1,0:T(8,128)(2,1)}, bf16[4,2,2,256,256]{4,3,2,1,0:T(8,128)(2,1)}, bf16[4,2,2,256,256]{4,3,2,1,0:T(8,128)(2,1)}) custom-call(bf16[128,8192]{1,0:T(8,128)(2,1)} %x.1, bf16[128,8192]{1,0:T(8,128)(2,1)} %c.1, bf16[32,2,32,256]{3,2,1,0:T(8,128)(2,1)} %w1.1, bf16[32,2,32,256]{3,2,1,0:T(8,128)(2,1)} %w2.1), custom_call_target="tpu_custom_call" | custom-call | tf_op jit(solution)/shard_map/bring/pallas_call | solution.py:187
  161.7 14.1 %factors.1 = (bf16[4,512,512]{2,1,0:T(8,128)(2,1)}, bf16[4,2,2,256,256]{4,3,2,1,0:T(8,128)(2,1)}, bf16[4,2,2,256,256]{4,3,2,1,0:T(8,128)(2,1)}) custom-call(s32[2,256]{1,0:T(2,128)} %order.1, bf16[4,512,512]{2,1,0:T(8,128)(2,1)} %get-tuple-element.13.x, bf16[4,512,512]{2,1,0:T(8,128)(2,1)} %get-tuple-element.14.c, ...), custom_call_target="tpu_custom_call" | custom-call | tf_op jit(solution)/shard_map/factors/pallas_call | solution.py:198
  175.8 115.2 %send_back.1 = (bf16[128,8192]{1,0:T(8,128)(2,1)}, bf16[2,32,2,32,256]{4,3,2,1,0:T(8,128)(2,1)}, bf16[2,32,2,32,256]{4,3,2,1,0:T(8,128)(2,1)}) custom-call(bf16[4,512,512]{2,1,0:T(8,128)(2,1)} %get-tuple-element.17.ig, bf16[4,2,2,256,256]{4,3,2,1,0:T(8,128)(2,1)} %get-tuple-element.18.gf, bf16[4,2,2,256,256]{4,3,2,1,0:T(8,128)(2,1)} %get-tuple-element.19.gs), custom_call_target="tpu_custom_call" | custom-call | tf_op jit(solution)/shard_map/send_back/pallas_call | solution.py:214
  291.0 0.0 copy-start
  291.0 5.9 %convert_reduce_fusion = (f32[32,2,32,256]{3,2,1,0:T(8,128)}, f32[32,2,32,256]{3,2,1,0:T(8,128)}) fusion(bf16[2,32,2,32,256]{4,3,2,1,0:T(8,128)(2,1)} %get-tuple-element.22, bf16[2,32,2,32,256]{4,3,2,1,0:T(8,128)(2,1)} %get-tuple-element.21), kind=kLoop, calls=%fused_computation | loop fusion | flops 3145728 | bytes 8388608 | tf_op jit(solution)/shard_map/reduce_sum | solution.py:223
  296.9 0.0 copy-done
  296.9 1.3 copy.9
Async XLA Ops:
  291.0 5.9 %copy-start = (bf16[128,8192]{1,0:T(8,128)(2,1)S(1)}, bf16[128,8192]{1,0:T(8,128)(2,1)}, u32[]{:S(2)}) copy-start(bf16[128,8192]{1,0:T(8,128)(2,1)} %get-tuple-element.28) | copy-start | bytes 6291460

commit v2 on v1

v2 whole, which is shorter than its diff:
```python
import functools
import math

import jax
import jax.numpy as jnp
from jax import lax
from jax.experimental import pallas as pl
from jax.experimental.pallas import tpu as pltpu
from jax.sharding import PartitionSpec as P

B = 256
MESH = pl.DeviceIdType.MESH
ANY = pl.BlockSpec(memory_space=pl.ANY)
NT = (((1,), (1,)), ((), ()))
TN = (((0,), (0,)), ((), ()))


class Plan:
    def __init__(self, dp, mp, local_blocks):
        self.dp, self.mp, self.nb = dp, mp, local_blocks
        self.low = mp // 4
        g = max(1, dp // 2)
        while local_blocks % (4 * g):
            g //= 2
        self.g, self.groups = g, dp // g
        self.nq = local_blocks // (4 * g)

    def here(self):
        d, m = lax.axis_index("dp"), lax.axis_index("mp")
        return d, d // self.g, d % self.g, m // self.low, m % self.low


def greet(plan, d, h, lo):
    barrier = pltpu.get_barrier_semaphore()
    others = 4 * plan.dp
    me = d * 4 + h
    for k in range(1, others):
        t = (me + k) % others
        pl.semaphore_signal(
            barrier, inc=1, device_id=(t // 4, (t % 4) * plan.low + lo), device_id_type=MESH
        )
    pl.semaphore_wait(barrier, others - 1)


def sweep(first, last, body):
    lax.fori_loop(first, last, lambda k, _: (body(k), None)[1], None)


def whole(plan, scale, order, x, c, w1, w2, igo, gfo, gso, xb, cb, w1b, w2b, ig, gf, gs, w1p, w2p, act, pre,
          ts, tr, ws, wr, ls, os, orr, gsem, gr, ol):
    d, gi, r, h, lo = plan.here()
    tok, rows, nq = x.shape[0], w1.shape[2], plan.nq
    n_t, n_w = 4 * plan.g, 4 * plan.dp
    me_o, me_w = r * 4 + h, d * 4 + h
    greet(plan, d, h, lo)

    def peer_of_group(t):
        return (gi * plan.g + t // 4, (t % 4) * plan.low + lo)

    def peer_of_all(t):
        return (t // 4, (t % 4) * plan.low + lo)

    def tokens_in(i, a, k):
        t = (me_o + k) % n_t
        src, dst = ((x, xb), (c, cb))[a]
        s = src.at[:, pl.ds(pl.multiple_of((t * nq + i) * B, B), B)]
        e = dst.at[i, h, pl.ds(pl.multiple_of(r * tok, tok), tok)]
        if isinstance(k, int) and k == 0:
            return pltpu.make_async_copy(s, e, ls.at[i, a])
        return pltpu.make_async_remote_copy(
            s, e, ts.at[i, a, k], tr.at[i, a, k], device_id=peer_of_group(t), device_id_type=MESH
        )

    def weights_in(i, a, k):
        t = (me_w + k) % n_w
        src, dst = ((w1, w1b), (w2, w2b))[a]
        o = ((t // 4) % plan.g) * 4 + t % 4
        s = src.at[o * nq + i]
        e = dst.at[i, h, :, pl.ds(pl.multiple_of(d * rows, rows), rows)]
        if isinstance(k, int) and k == 0:
            return pltpu.make_async_copy(s, e, ls.at[i, 2 + a])
        return pltpu.make_async_remote_copy(
            s, e, ws.at[i, a, k], wr.at[i, a, k], device_id=peer_of_all(t), device_id_type=MESH
        )

    def tokens_out(i, k):
        t = (me_o + k) % n_t
        s = ig.at[i, t % 4, pl.ds(pl.multiple_of((t // 4) * tok, tok), tok)]
        e = igo.at[:, pl.ds(pl.multiple_of((me_o * nq + i) * B, B), B)]
        if isinstance(k, int) and k == 0:
            return pltpu.make_async_copy(s, e, ol.at[i, 0])
        return pltpu.make_async_remote_copy(
            s, e, os.at[i, k], orr.at[i, k], device_id=peer_of_group(t), device_id_type=MESH
        )

    def grads_out(i, a, k):
        t = (me_w + k) % n_w
        src, dst = ((gf, gfo), (gs, gso))[a]
        s = src.at[i, t % 4, :, pl.ds(pl.multiple_of((t // 4) * rows, rows), rows)]
        e = dst.at[gi, me_o * nq + i]
        if isinstance(k, int) and k == 0:
            return pltpu.make_async_copy(s, e, ol.at[i, 1 + a])
        return pltpu.make_async_remote_copy(
            s, e, gsem.at[i, a, k], gr.at[i, a, k], device_id=peer_of_all(t), device_id_type=MESH
        )

    def all_in(i, act_on):
        def near(k):
            for a in (0, 1):
                act_on(weights_in(i, a, k))
                act_on(tokens_in(i, a, k))

        def far(k):
            for a in (0, 1):
                act_on(weights_in(i, a, k))

        sweep(1, n_t, near)
        sweep(n_t, n_w, far)

    def all_out(i, act_on):
        def near(k):
            act_on(grads_out(i, 0, k))
            act_on(grads_out(i, 1, k))
            act_on(tokens_out(i, k))

        def far(k):
            act_on(grads_out(i, 0, k))
            act_on(grads_out(i, 1, k))

        sweep(1, n_t, near)
        sweep(n_t, n_w, far)

    def own_in(i):
        return [f(i, a, 0) for f in (tokens_in, weights_in) for a in (0, 1)]

    def own_out(i):
        return [tokens_out(i, 0), grads_out(i, 0, 0), grads_out(i, 1, 0)]

    for i in range(nq):
        all_in(i, lambda copy: copy.start())
        for copy in own_in(i):
            copy.start()
    for i in range(nq):
        for copy in own_in(i):
            copy.wait()
        all_in(i, lambda copy: copy.wait_recv())
        factors(scale, order, xb.at[i], cb.at[i], w1b.at[i], w2b.at[i], ig.at[i], gf.at[i], gs.at[i], w1p, w2p, act, pre)
        all_out(i, lambda copy: copy.start())
        for copy in own_out(i):
            copy.start()
    for i in range(nq):
        all_in(i, lambda copy: copy.wait_send())
        for copy in own_out(i):
            copy.wait()
        all_out(i, lambda copy: copy.wait())


def dot(left, right, dims=(((1,), (0,)), ((), ()))):
    return lax.dot_general(left, right, dims, preferred_element_type=jnp.float32)


def factors(scale, order, x, c, w1, w2, ig, gf, gs, w1p, w2p, act, pre):
    bf = jnp.bfloat16
    place = lax.broadcasted_iota(jnp.int32, (B, B), 0)
    spread_one = (place == order[0:1, :]).astype(jnp.float32).astype(bf)
    spread_two = (place == order[1:2, :]).astype(jnp.float32).astype(bf)
    root = math.sqrt(2.0 / math.pi)
    for h in range(4):
        w1p[h] = dot(spread_one, w1[h, 1]).astype(bf)
        w2p[h] = dot(spread_two, w2[h, 1]).astype(bf)
    for h in range(4):
        p, q = h ^ 2, h ^ 1
        v = dot(x[h], w1[h, 0]) + dot(x[p], w1p[h])
        up = dot(c[h], w2[h, 0], NT) + dot(c[q], w2p[q], NT)
        v2 = v * v
        t = jnp.tanh(root * v * (1.0 + 0.044715 * v2))
        half = 0.5 + 0.5 * t
        act[h] = (v * half).astype(bf)
        slope = half + (0.5 * root) * v * (1.0 - t * t) * (1.0 + (3 * 0.044715) * v2)
        pre[h] = (up * slope).astype(bf)
    for h in range(4):
        p, q = h ^ 2, h ^ 1
        ig[h] = (dot(pre[h], w1[h, 0], NT) + dot(pre[p], w1p[p], NT)).astype(bf)
        gf[h, 0] = (dot(x[h], pre[h], TN) * scale).astype(bf)
        cross = (dot(x[p], pre[h], TN) * scale).astype(bf)
        gf[h, 1] = dot(spread_one, cross, TN).astype(bf)
        gs[h, 0] = (dot(act[h], c[h], TN) * scale).astype(bf)
        cross = (dot(act[q], c[h], TN) * scale).astype(bf)
        gs[h, 1] = dot(spread_two, cross, TN).astype(bf)


def shards(plan, inputs, cotangent, first_weight, second_weight, orders):
    tok, width = inputs.shape
    rows = first_weight.shape[2]
    bf = jnp.bfloat16
    all_tok = plan.g * tok
    nq = plan.nq
    scale = 1.0 / math.sqrt(tok * plan.dp)
    dma = pltpu.SemaphoreType.DMA
    n_t, n_w = 4 * plan.g, 4 * plan.dp
    toks = pltpu.VMEM((nq, 4, all_tok, B), bf)
    mats = pltpu.VMEM((nq, 4, 2, B, B), bf)
    part = jax.ShapeDtypeStruct((plan.groups, plan.nb, 2, rows, B), bf)
    input_grad, first, second = pl.pallas_call(
        functools.partial(whole, plan, scale),
        out_shape=(jax.ShapeDtypeStruct((tok, width), bf), part, part),
        in_specs=[pl.BlockSpec(memory_space=pltpu.VMEM)] + [ANY] * 4,
        out_specs=(ANY,) * 3,
        scratch_shapes=[toks, toks, mats, mats, toks, mats, mats]
        + [pltpu.VMEM((4, B, B), bf)] * 2
        + [pltpu.VMEM((4, all_tok, B), bf)] * 2
        + [dma((nq, 2, n_t)), dma((nq, 2, n_t)), dma((nq, 2, n_w)), dma((nq, 2, n_w)), dma((nq, 4))]
        + [dma((nq, n_t)), dma((nq, n_t)), dma((nq, 2, n_w)), dma((nq, 2, n_w)), dma((nq, 3))],
        compiler_params=pltpu.CompilerParams(
            collective_id=0, has_side_effects=True, vmem_limit_bytes=56 * 2**20
        ),
        name="whole",
    )(orders, inputs, cotangent, first_weight, second_weight)
    total = lambda parts: jnp.sum(parts.astype(jnp.float32), axis=0)
    return input_grad, total(first), total(second)


def solution(mesh):
    in_specs = (
        P("dp", "mp"),
        P("dp", "mp"),
        P("mp", None, "dp", None),
        P("mp", None, "dp", None),
        P(),
    )
    out_specs = (P("dp", "mp"), P("mp", None, "dp", None), P("mp", None, "dp", None))

    def body(inputs, *rest):
        plan = Plan(mesh.shape["dp"], mesh.shape["mp"], inputs.shape[1] // B)
        return shards(plan, inputs, *rest)

    return jax.shard_map(body, mesh=mesh, in_specs=in_specs, out_specs=out_specs, check_vma=False)
```

time: 298 us -> 252 us (0.85)
  Pallas kernels: 290 us -> 244 us
    pallas_call x3 -> x1, Pallas kernels: 290 us -> 244 us  [shards(): pl.pallas_call(functools.partial(whole, plan, scale), out_shape=(jax.Shap...]
where the time goes in v2:
time: 252 us
  Pallas kernels  244 us (97%)
  other arithmetic  5.88 us (2%)
    pallas_call x1, Pallas kernels, shards(): pl.pallas_call(functools.partial(whole, plan, scale), out_shape=(jax.Shap...  244 us
    reduce_sum x1, other arithmetic, shards(): total = lambda parts: jnp.sum(parts.astype(jnp.float32), axis=0)  5.88 us

profile of v2, /device:TPU:31, one launch (start us, length us, event | category | flops | bytes accessed | tf_op | source)
XLA Modules:
  0.0 252.0 jit_solution(8421874418412950128)
XLA Ops:
  0.6 244.1 %whole.1 = (bf16[128,8192]{1,0:T(8,128)(2,1)}, bf16[2,32,2,32,256]{4,3,2,1,0:T(8,128)(2,1)}, bf16[2,32,2,32,256]{4,3,2,1,0:T(8,128)(2,1)}) custom-call(s32[2,256]{1,0:T(2,128)} %order.1, bf16[128,8192]{1,0:T(8,128)(2,1)} %x.1, bf16[128,8192]{1,0:T(8,128)(2,1)} %c.1, bf16[32,2,32,256]{3,2,1,0:T(8,128)(2,1)} %w1.1, bf16[32,2,32,256]{3,2,1,0:T(8,128)(2,1)} %w2.1), custom_call_target="tpu_custom_call" | custom-call | tf_op jit(solution)/shard_map/whole/pallas_call | solution.py:204
  244.8 0.0 copy-start
  244.8 5.9 %convert_reduce_fusion = (f32[32,2,32,256]{3,2,1,0:T(8,128)}, f32[32,2,32,256]{3,2,1,0:T(8,128)}) fusion(bf16[2,32,2,32,256]{4,3,2,1,0:T(8,128)(2,1)} %get-tuple-element.8, bf16[2,32,2,32,256]{4,3,2,1,0:T(8,128)(2,1)} %get-tuple-element.7), kind=kLoop, calls=%fused_computation | loop fusion | flops 3145728 | bytes 8388608 | tf_op jit(solution)/shard_map/reduce_sum | solution.py:219
  250.7 0.0 copy-done
  250.7 1.3 copy.9
Async XLA Ops:
  244.8 5.9 %copy-start = (bf16[128,8192]{1,0:T(8,128)(2,1)S(1)}, bf16[128,8192]{1,0:T(8,128)(2,1)}, u32[]{:S(2)}) copy-start(bf16[128,8192]{1,0:T(8,128)(2,1)} %get-tuple-element.14) | copy-start | bytes 6291460

commit v3 on v2

--- a/solution.py
+++ b/solution.py
@@ -61,7 +61,7 @@
         return (t // 4, (t % 4) * plan.low + lo)
 
     def tokens_in(i, a, k):
-        t = (me_o + k) % n_t
+        t = (me_o + 5 * k) % n_t
         src, dst = ((x, xb), (c, cb))[a]
         s = src.at[:, pl.ds(pl.multiple_of((t * nq + i) * B, B), B)]
         e = dst.at[i, h, pl.ds(pl.multiple_of(r * tok, tok), tok)]
@@ -72,7 +72,7 @@
         )
 
     def weights_in(i, a, k):
-        t = (me_w + k) % n_w
+        t = (me_w + 11 * k) % n_w
         src, dst = ((w1, w1b), (w2, w2b))[a]
         o = ((t // 4) % plan.g) * 4 + t % 4
         s = src.at[o * nq + i]
@@ -84,7 +84,7 @@
         )
 
     def tokens_out(i, k):
-        t = (me_o + k) % n_t
+        t = (me_o + 5 * k) % n_t
         s = ig.at[i, t % 4, pl.ds(pl.multiple_of((t // 4) * tok, tok), tok)]
         e = igo.at[:, pl.ds(pl.multiple_of((me_o * nq + i) * B, B), B)]
         if isinstance(k, int) and k == 0:
@@ -94,7 +94,7 @@
         )
 
     def grads_out(i, a, k):
-        t = (me_w + k) % n_w
+        t = (me_w + 11 * k) % n_w
         src, dst = ((gf, gfo), (gs, gso))[a]
         s = src.at[i, t % 4, :, pl.ds(pl.multiple_of((t // 4) * rows, rows), rows)]
         e = dst.at[gi, me_o * nq + i]
@@ -105,30 +105,31 @@
         )
 
     def all_in(i, act_on):
-        def near(k):
-            for a in (0, 1):
-                act_on(weights_in(i, a, k))
-                act_on(tokens_in(i, a, k))
-
-        def far(k):
-            for a in (0, 1):
-                act_on(weights_in(i, a, k))
-
-        sweep(1, n_t, near)
-        sweep(n_t, n_w, far)
+        def some_weights(k, first):
+            for j in range(first, plan.groups):
+                for a in (0, 1):
+                    act_on(weights_in(i, a, plan.groups * k + j))
+
+        def both(k):
+            act_on(tokens_in(i, 0, k))
+            some_weights(k, 0)
+            act_on(tokens_in(i, 1, k))
+
+        some_weights(0, 1)
+        sweep(1, n_t, both)
 
     def all_out(i, act_on):
-        def near(k):
-            act_on(grads_out(i, 0, k))
-            act_on(grads_out(i, 1, k))
+        def some_grads(k, first):
+            for j in range(first, plan.groups):
+                for a in (0, 1):
+                    act_on(grads_out(i, a, plan.groups * k + j))
+
+        def both(k):
             act_on(tokens_out(i, k))
-
-        def far(k):
-            act_on(grads_out(i, 0, k))
-            act_on(grads_out(i, 1, k))
-
-        sweep(1, n_t, near)
-        sweep(n_t, n_w, far)
+            some_grads(k, 0)
+
+        some_grads(0, 1)
+        sweep(1, n_t, both)
 
     def own_in(i):
         return [f(i, a, 0) for f in (tokens_in, weights_in) for a in (0, 1)]

time: 252 us -> 227 us (0.901); the launches traced: 252 us -> 223 us
  Pallas kernels: 244 us -> 215 us
    pallas_call x1, Pallas kernels: 244 us -> 215 us  [shards(): pl.pallas_call(functools.partial(whole, plan, scale), out_shape=(jax.Shap...]
where the time goes in v3:
time: 227 us; the launch traced here: 223 us
  Pallas kernels  215 us (95%)
  other arithmetic  5.88 us (3%)
    pallas_call x1, Pallas kernels, shards(): pl.pallas_call(functools.partial(whole, plan, scale), out_shape=(jax.Shap...  215 us
    reduce_sum x1, other arithmetic, shards(): total = lambda parts: jnp.sum(parts.astype(jnp.float32), axis=0)  5.88 us

profile of v3, /device:TPU:31, one launch (start us, length us, event | category | flops | bytes accessed | tf_op | source)
XLA Modules:
  0.0 223.0 jit_solution(8117584210004452298)
XLA Ops:
  0.6 215.1 %whole.1 = (bf16[128,8192]{1,0:T(8,128)(2,1)}, bf16[2,32,2,32,256]{4,3,2,1,0:T(8,128)(2,1)}, bf16[2,32,2,32,256]{4,3,2,1,0:T(8,128)(2,1)}) custom-call(s32[2,256]{1,0:T(2,128)} %order.1, bf16[128,8192]{1,0:T(8,128)(2,1)} %x.1, bf16[128,8192]{1,0:T(8,128)(2,1)} %c.1, bf16[32,2,32,256]{3,2,1,0:T(8,128)(2,1)} %w1.1, bf16[32,2,32,256]{3,2,1,0:T(8,128)(2,1)} %w2.1), custom_call_target="tpu_custom_call" | custom-call | tf_op jit(solution)/shard_map/whole/pallas_call | solution.py:205
  215.8 0.0 copy-start
  215.8 5.9 %convert_reduce_fusion = (f32[32,2,32,256]{3,2,1,0:T(8,128)}, f32[32,2,32,256]{3,2,1,0:T(8,128)}) fusion(bf16[2,32,2,32,256]{4,3,2,1,0:T(8,128)(2,1)} %get-tuple-element.8, bf16[2,32,2,32,256]{4,3,2,1,0:T(8,128)(2,1)} %get-tuple-element.7), kind=kLoop, calls=%fused_computation | loop fusion | flops 3145728 | bytes 8388608 | tf_op jit(solution)/shard_map/reduce_sum | solution.py:220
  221.7 0.0 copy-done
  221.7 1.3 copy.9
Async XLA Ops:
  215.8 5.9 %copy-start = (bf16[128,8192]{1,0:T(8,128)(2,1)S(1)}, bf16[128,8192]{1,0:T(8,128)(2,1)}, u32[]{:S(2)}) copy-start(bf16[128,8192]{1,0:T(8,128)(2,1)} %get-tuple-element.14) | copy-start | bytes 6291460

commit v4 on v3

--- a/solution.py
+++ b/solution.py
@@ -190,6 +190,12 @@
         gs[h, 1] = dot(spread_two, cross, TN).astype(bf)
 
 
+def finish(one, two, grad, first, second, out):
+    first[...] = jnp.sum(one[...].astype(jnp.float32), axis=0)
+    second[...] = jnp.sum(two[...].astype(jnp.float32), axis=0)
+    out[...] = grad[...]
+
+
 def shards(plan, inputs, cotangent, first_weight, second_weight, orders):
     tok, width = inputs.shape
     rows = first_weight.shape[2]
@@ -217,8 +223,22 @@
         ),
         name="whole",
     )(orders, inputs, cotangent, first_weight, second_weight)
-    total = lambda parts: jnp.sum(parts.astype(jnp.float32), axis=0)
-    return input_grad, total(first), total(second)
+    steps = math.gcd(plan.nb, tok // 16, 8)
+    each = plan.nb // steps
+    part_spec = pl.BlockSpec((plan.groups, each, 2, rows, B), lambda i: (0, i, 0, 0, 0))
+    sum_spec = pl.BlockSpec((each, 2, rows, B), lambda i: (i, 0, 0, 0))
+    grad_spec = pl.BlockSpec((tok // steps, width), lambda i: (i, 0))
+    summed = jax.ShapeDtypeStruct((plan.nb, 2, rows, B), jnp.float32)
+    first, second, input_grad = pl.pallas_call(
+        finish,
+        grid=(steps,),
+        out_shape=(summed, summed, jax.ShapeDtypeStruct((tok, width), bf)),
+        in_specs=[part_spec, part_spec, grad_spec],
+        out_specs=(sum_spec, sum_spec, grad_spec),
+        compiler_params=pltpu.CompilerParams(vmem_limit_bytes=56 * 2**20),
+        name="finish",
+    )(first, second, input_grad)
+    return input_grad, first, second
 
 
 def solution(mesh):

time: 227 us -> 228 us (level)
  Pallas kernels: 215 us -> 223 us
  other arithmetic: 5.88 us -> 0 us
    pallas_call x0 -> x1, Pallas kernels: none -> 7.71 us  [shards(): pl.pallas_call(finish, grid=(steps,), out_shape=(summed, summed, jax.Shap...]
    reduce_sum x1 -> x0, other arithmetic: 5.88 us -> none  [shards(): total = lambda parts: jnp.sum(parts.astype(jnp.float32), axis=0)]
where the time goes in v4:
time: 228 us; the launch traced here: 223 us
  Pallas kernels  223 us (98%)
    pallas_call x1, Pallas kernels, shards(): pl.pallas_call(functools.partial(whole, plan, scale), out_shape=(jax.Shap...  215 us
    pallas_call x1, Pallas kernels, shards(): pl.pallas_call(finish, grid=(steps,), out_shape=(summed, summed, jax.Shap...  7.71 us

profile of v4, /device:TPU:31, one launch (start us, length us, event | category | flops | bytes accessed | tf_op | source)
XLA Modules:
  0.0 223.5 jit_solution(9732418361764998519)
XLA Ops:
  0.6 215.1 %whole.1 = (bf16[128,8192]{1,0:T(8,128)(2,1)}, bf16[2,32,2,32,256]{4,3,2,1,0:T(8,128)(2,1)}, bf16[2,32,2,32,256]{4,3,2,1,0:T(8,128)(2,1)}) custom-call(s32[2,256]{1,0:T(2,128)} %order.1, bf16[128,8192]{1,0:T(8,128)(2,1)} %x.1, bf16[128,8192]{1,0:T(8,128)(2,1)} %c.1, bf16[32,2,32,256]{3,2,1,0:T(8,128)(2,1)} %w1.1, bf16[32,2,32,256]{3,2,1,0:T(8,128)(2,1)} %w2.1), custom_call_target="tpu_custom_call" | custom-call | tf_op jit(solution)/shard_map/whole/pallas_call | solution.py:211
  215.8 7.7 %finish.1 = (f32[32,2,32,256]{3,2,1,0:T(8,128)}, f32[32,2,32,256]{3,2,1,0:T(8,128)}, bf16[128,8192]{1,0:T(8,128)(2,1)}) custom-call(bf16[2,32,2,32,256]{4,3,2,1,0:T(8,128)(2,1)} %get-tuple-element.9.one, bf16[2,32,2,32,256]{4,3,2,1,0:T(8,128)(2,1)} %get-tuple-element.10.two, bf16[128,8192]{1,0:T(8,128)(2,1)} %get-tuple-element.11.grad), custom_call_target="tpu_custom_call" | custom-call | tf_op jit(solution)/shard_map/finish/pallas_call | solution.py:232
